TPU v7x, 32 devices: a whole 2x2x4 slice. The times are simulated.
32 devices in a mesh: parts: 2 (over y), tm: 4 (over z), rows: 2 (over x), cols: 2 (over core).
Axes of the slice: x: 2, y: 2, z: 4, core: 2. Of those that a mesh axis runs over, the one named last changes fastest.
Arguments:
- frames: bfloat16 [256, 256, 512], P(('parts', 'tm'), 'rows', 'cols'), parts along dimension 0, may hold values from -6 to 6
- transfer: bfloat16 [256, 128, 128], P(('parts', 'tm')), parts along dimension 0, may hold values from 0.099609375 to 1
- cutoff: int32 [128, 128], replicated, may hold values from 0 to 64
Outputs:
- restored: float32 [256, 256, 512], P(('parts', 'tm'), 'rows', 'cols'), parts along dimension 0
There are 2 independent parts, one for each index of `parts`. A program takes and returns all parts, laid end to end along the dimension named above; an argument that names none is the same for every part. Nothing has to cross between parts.
Inputs may be any that keep to these rules, and one draw needn't show every extreme that they name: cutoff[u, v] is the largest value of min(w, 128 - w) kept at wavenumber (u, v).
All inputs are finite; a program needn't handle non-finite values.
Results may differ from a plain program's by a relative error of at most 0.0003.
Values may be sent and summed in bfloat16 or wider, within the bound.
No kernel may reach another device: no remote copies, remote signals or barrier semaphores. Data moves between devices by JAX's collectives and lax.ppermute only.
A program may use at most 128 MiB of HBM per device.

v0:
```python
import math
import jax
import jax.numpy as jnp
from jax import lax
from jax.sharding import PartitionSpec as P

noise_level = 0.05


def with_halo(cells, sides, width):
    for axis, dim in sides:
        count = lax.axis_size(axis)
        ends = count - 1
        head = lax.slice_in_dim(cells, 0, width, axis=dim)
        tail = lax.slice_in_dim(cells, cells.shape[dim] - width, cells.shape[dim], axis=dim)
        cells = jnp.concatenate(
            [
                lax.ppermute(tail, axis, [(i, (i + 1) % count) for i in range(ends)]),
                cells,
                lax.ppermute(head, axis, [((i + 1) % count, i) for i in range(ends)]),
            ],
            axis=dim,
        )
    return cells


def tables(length):
    series = jnp.arange(length, dtype=jnp.int32)
    product = series[:, None] * series[None, :] % length
    angles = product.astype(jnp.float32) * (2.0 * math.pi / length)
    return (jnp.cos(angles), jnp.sin(angles))


def forward_spatial(images, cos_space, sin_space):
    highest = lax.Precision.HIGHEST
    factor = 1.0 / cos_space.shape[0]
    row_real = jnp.einsum("cnab,bv->cnav", images, cos_space, precision=highest)
    row_imag = -jnp.einsum("cnab,bv->cnav", images, sin_space, precision=highest)
    spec_real = (
        jnp.einsum("ua,cnav->cnuv", cos_space, row_real, precision=highest)
        + jnp.einsum("ua,cnav->cnuv", sin_space, row_imag, precision=highest)
    ) * factor
    spec_imag = (
        jnp.einsum("ua,cnav->cnuv", cos_space, row_imag, precision=highest)
        - jnp.einsum("ua,cnav->cnuv", sin_space, row_real, precision=highest)
    ) * factor
    return (spec_real, spec_imag)


def inverse_spatial(spec_real, spec_imag, cos_space, sin_space):
    highest = lax.Precision.HIGHEST
    factor = 1.0 / cos_space.shape[0]
    col_real = jnp.einsum("au,cnuv->cnav", cos_space, spec_real, precision=highest) - jnp.einsum(
        "au,cnuv->cnav", sin_space, spec_imag, precision=highest
    )
    col_imag = jnp.einsum("au,cnuv->cnav", cos_space, spec_imag, precision=highest) + jnp.einsum(
        "au,cnuv->cnav", sin_space, spec_real, precision=highest
    )
    return (
        jnp.einsum("cnav,vb->cnab", col_real, cos_space, precision=highest)
        - jnp.einsum("cnav,vb->cnab", col_imag, sin_space, precision=highest)
    ) * factor


def join(spec_real, spec_imag, gains, count):
    numerator_real = jnp.zeros(spec_real.shape[:1] + (count,) + spec_real.shape[2:], jnp.float32)
    numerator_imag = jnp.zeros_like(numerator_real)
    denominator = jnp.zeros(gains.shape[:1] + (count,) + gains.shape[2:], jnp.float32)
    for offset in range(5):
        gain = lax.slice_in_dim(gains, offset, offset + count, axis=1)
        numerator_real = numerator_real + gain * lax.slice_in_dim(
            spec_real, offset, offset + count, axis=1
        )
        numerator_imag = numerator_imag + gain * lax.slice_in_dim(
            spec_imag, offset, offset + count, axis=1
        )
        denominator = denominator + gain * gain
    denominator = denominator + noise_level
    return (numerator_real / denominator, numerator_imag / denominator)


def temporal(stacked, cutoff_local, channels):
    highest = lax.Precision.HIGHEST
    time_len = stacked.shape[1]
    cos_time, sin_time = tables(time_len)
    factor = 1.0 / math.sqrt(time_len)
    real = stacked[:channels]
    imag = stacked[channels:]
    freq_real = (
        jnp.einsum("wt,stk->swk", cos_time, real, precision=highest)
        + jnp.einsum("wt,stk->swk", sin_time, imag, precision=highest)
    ) * factor
    freq_imag = (
        jnp.einsum("wt,stk->swk", cos_time, imag, precision=highest)
        - jnp.einsum("wt,stk->swk", sin_time, real, precision=highest)
    ) * factor
    omega = jnp.arange(time_len, dtype=jnp.int32)
    distance = jnp.minimum(omega, time_len - omega)
    keeper = (distance[:, None] <= cutoff_local[None, :])[None]
    freq_real = jnp.where(keeper, freq_real, 0.0)
    freq_imag = jnp.where(keeper, freq_imag, 0.0)
    back_real = (
        jnp.einsum("tw,swk->stk", cos_time, freq_real, precision=highest)
        - jnp.einsum("tw,swk->stk", sin_time, freq_imag, precision=highest)
    ) * factor
    back_imag = (
        jnp.einsum("tw,swk->stk", cos_time, freq_imag, precision=highest)
        + jnp.einsum("tw,swk->stk", sin_time, freq_real, precision=highest)
    ) * factor
    return jnp.concatenate([back_real, back_imag], axis=0)


def to_channels(images, side, across):
    total = images.shape[0]
    return images.reshape(total, side, across, side).transpose(2, 0, 1, 3)


def on_device(frames, transfer, cutoff):
    count = frames.shape[0]
    side = transfer.shape[1]
    across = frames.shape[2] // side
    cos_space, sin_space = tables(side)
    packed = jnp.concatenate([frames, transfer], axis=2)
    extended = with_halo(packed, (("tm", 0),), 2)
    images = to_channels(extended[:, :, : across * side].astype(jnp.float32), side, across)
    spec_real, spec_imag = forward_spatial(images, cos_space, sin_space)
    gains = extended[:, :, across * side :].astype(jnp.float32)[None]
    joined_real, joined_imag = join(spec_real, spec_imag, gains, count)
    payload = jnp.concatenate([joined_real, joined_imag], axis=0).reshape(
        2 * across, count, side * side
    )
    gathered = lax.all_to_all(payload, "tm", split_axis=2, concat_axis=1, tiled=True)
    width = gathered.shape[2]
    start = lax.axis_index("tm") * width
    cutoff_local = lax.dynamic_slice_in_dim(cutoff.reshape(-1), start, width)
    filtered = temporal(gathered, cutoff_local, across)
    returned = lax.all_to_all(filtered, "tm", split_axis=1, concat_axis=2, tiled=True)
    spectra_back = returned.reshape(2 * across, count, side, side)
    result = inverse_spatial(spectra_back[:across], spectra_back[across:], cos_space, sin_space)
    return result.transpose(1, 2, 0, 3).reshape(count, side, across * side)


def solution(mesh):
    return jax.shard_map(
        on_device,
        mesh=mesh,
        in_specs=(P(("parts", "tm"), "rows", "cols"), P(("parts", "tm"), None, None), P()),
        out_specs=P(("parts", "tm"), "rows", "cols"),
        check_vma=False,
    )
```

profile of v0, /device:TPU:0, one launch (start us, length us, event | category | flops | bytes accessed | tf_op | source)
XLA Modules:
  0.0 778.8 jit_solution(10579485411199657045)
XLA Ops:
  0.0 3.2 copy.61
  3.2 2.2 copy.62
  5.5 5.0 collective-permute-start
  11.8 2.8 collective-permute-done
  14.6 4.1 collective-permute-done.1
  20.3 3.0 copy.63
  23.4 2.3 fusion.30
  27.9 7.9 %fusion.10 = f32[2,36,128,128]{3,2,1,0:T(8,128)S(1)} fusion(f32[2,36,128,128]{3,2,1,0:T(8,128)S(1)} %fusion.30), kind=kOutput, calls=%fused_computation.18 | convolution fusion | flops 1813348352 | bytes 9437184 | tf_op jit(solution)/shard_map/ua,cnav->cnuv/dot_general | solution.py:44
  35.8 7.7 fusion.12
  43.5 4.8 multiply_bitcast_fusion
  48.3 4.4 multiply_bitcast_fusion.1
  54.4 11.6 %slice_bitcast_fusion.4 = (f32[32,128,128]{1,2,0:T(8,128)}, f32[32,128,128]{1,2,0:T(8,128)}, f32[32,128,128]{1,2,0:T(8,128)}, f32[32,128,128]{1,2,0:T(8,128)}, f...) fusion(f32[1,36,128,128]{2,3,1,0:T(8,128)} %fusion.36), kind=kLoop, calls=%fused_computation.61 | loop fusion | flops 5242880 | bytes 23068672 | tf_op jit(solution)/shard_map/mul | solution.py:71
  66.0 9.8 %fusion.20 = (f32[2,32,128,128]{2,3,1,0:T(8,128)S(1)}, f32[2,32,128,128]{2,3,1,0:T(8,128)}) fusion(f32[2,36,128,128]{2,3,1,0:T(8,128)S(1)} %multiply_bitcast_fusion.1, f32[32,128,128]{1,2,0:T(8,128)} %get-tuple-element.14, f32[32,128,128]{1,2,0:T(8,128)} %get-tuple-element.15, f32[32,128,128]{1,2,0:T(8,128)} %get-tuple-element.16, ...), kind=kLoop, calls=%fused_computation.34 | loop fusion | flops 20971520 | bytes 62914560 | tf_op jit(solution)/shard_map/div | solution.py:79
  75.8 6.2 pad_maximum_fusion
  82.0 26.7 %copy.146 = f32[4,32,128,128]{1,0,3,2:T(4,128)} copy(f32[4,32,128,128]{2,3,1,0:T(8,128)} %pad_maximum_fusion) | data formatting | bytes 16777216 | tf_op jit(solution)/shard_map/reshape | solution.py:129
  108.7 41.7 %reshape.77 = f32[4,1,524288]{2,1,0:T(1,128)} reshape(f32[16384,4,32]{2,1,0:T(4,128)} %bitcast.139) | data formatting | bytes 16777216
  150.4 5.6 all-to-all-start
  158.7 179.6 %all-to-all-done = f32[4,1,524288]{2,1,0:T(1,128)} async-done(((f32[4,1,524288]{2,1,0:T(1,128)}), f32[4,1,524288]{2,1,0:T(1,128)}, u32[]{:S(2)}, u32[]{:S(2)}) %all-to-all-start) | async-done | bytes 8388640 | tf_op jit(solution)/shard_map/all_to_all | solution.py:132
  338.8 28.4 %reduce = f32[4,524288]{1,0:T(4,128)} reduce(f32[4,1,524288]{2,1,0:T(1,128)} %all-to-all-done, f32[]{:T(128)} %broadcast.190), dimensions={1}, to_apply=%all_to_all.22.reduce_sub_computation | reduce | bytes 16777220 | tf_op jit(solution)/shard_map/all_to_all | solution.py:132
  367.2 47.7 %reshape.78 = f32[16384,4,32]{2,1,0:T(4,128)} reshape(f32[4,524288]{1,0:T(4,128)} %reduce) | data formatting | bytes 16777216
  415.0 28.8 %copy.147 = f32[4,32,4,4096]{3,2,1,0:T(4,128)} copy(f32[4,32,4,4096]{1,0,3,2:T(4,128)} %bitcast.140) | data formatting | bytes 16777216 | tf_op jit(solution)/shard_map/all_to_all | solution.py:132
  443.8 4.0 fusion.174
  447.9 2.4 copy.77
  450.3 6.8 fusion.50
  457.1 2.6 copy.80
  459.8 6.8 fusion.46
  466.6 7.3 fusion.9
  473.9 3.7 fusion.48
  477.5 7.0 fusion.6
  484.6 3.7 fusion.44
  488.2 3.7 fusion.3
  491.9 4.1 fusion.1
  496.0 3.8 pad_maximum_fusion.1
  499.8 10.3 %copy.91 = f32[4,128,4096]{2,0,1:T(4,128)} copy(f32[4,128,4096]{1,2,0:T(8,128)} %pad_maximum_fusion.1) | data formatting | bytes 16777216 | tf_op jit(solution)/shard_map/concatenate | solution.py:110
  510.1 186.7 %all_to_all.30 = f32[4,128,4096]{2,0,1:T(4,128)S(1)} all-to-all(f32[4,128,4096]{2,0,1:T(4,128)} %copy.91), channel_id=1, replica_groups=mesh['parts'=2,'tm'=4,'rows'=2,'cols'=2] {'tm'}, dimensions={1} | all-to-all | bytes 16777216 | tf_op jit(solution)/shard_map/all_to_all | solution.py:137
  696.7 4.9 copy.92
  701.6 2.8 fusion.173
  704.4 4.7 copy.96
  709.0 6.1 slice.107
  715.1 10.3 %fusion.61 = f32[2,32,128,128]{3,2,1,0:T(8,128)} fusion(f32[2,32,128,128]{3,2,1,0:T(8,128)} %slice.107), kind=kOutput, calls=%fused_computation.94 | convolution fusion | flops 1610842112 | bytes 8388608 | tf_op jit(solution)/shard_map/au,cnuv->cnav/dot_general | solution.py:56
  725.5 8.6 %fusion.55 = f32[2,32,128,128]{3,2,1,0:T(8,128)} fusion(f32[2,32,128,128]{3,2,1,0:T(8,128)S(1)} %copy-done), kind=kOutput, calls=%fused_computation.88 | convolution fusion | flops 1610842112 | bytes 8388608 | tf_op jit(solution)/shard_map/au,cnuv->cnav/dot_general | solution.py:53
  734.1 4.7 copy.93
  738.8 6.1 slice.105
  744.9 9.3 %fusion.53 = f32[2,32,128,128]{3,2,1,0:T(8,128)S(1)} fusion(f32[2,32,128,128]{3,2,1,0:T(8,128)} %slice.105), kind=kOutput, calls=%fused_computation.86 | convolution fusion | flops 1610842112 | bytes 8388608 | tf_op jit(solution)/shard_map/au,cnuv->cnav/dot_general | solution.py:56
  754.2 7.0 fusion.63
  761.2 4.3 fusion.24
  765.6 4.9 multiply_bitcast_fusion.2
  772.7 5.6 copy.106
  (28 shorter events, 12.1 us)
Async XLA Ops:
  3.2 17.1 %copy-start.2 = (bf16[32,128,256]{1,2,0:T(8,128)(2,1)}, bf16[32,128,256]{1,2,0:T(8,128)(2,1)S(1)}, u32[]{:S(2)}) copy-start(bf16[32,128,256]{1,2,0:T(8,128)(2,1)S(1)} %copy.61) | copy-start | bytes 6291460
  5.5 14.8 %copy-start.5 = (bf16[32,128,128]{1,2,0:T(8,128)(2,1)}, bf16[32,128,128]{1,2,0:T(8,128)(2,1)S(1)}, u32[]{:S(2)}) copy-start(bf16[32,128,128]{1,2,0:T(8,128)(2,1)S(1)} %copy.62) | copy-start | bytes 3145732
  5.5 9.1 %collective-permute-start = (bf16[2,128,384]{1,2,0:T(8,128)(2,1)S(1)}, bf16[2,128,384]{1,2,0:T(8,128)(2,1)S(1)}, u32[]{:S(2)}, u32[]{:S(2)}) collective-permute-start(bf16[2,128,384]{1,2,0:T(8,128)(2,1)S(1)} %get-tuple-element.11), channel_id=1, source_target_pairs={{0,4},{4,8},{8,12},{1,5},{5,9},{9,13},{2,6},{6,10},{10,14},{3,7},{... | collective-permute-start | bytes 589832 | tf_op jit(solution)/shard_map/ppermute | solution.py:18
  10.5 8.3 %collective-permute-start.1 = (bf16[2,128,384]{1,2,0:T(8,128)(2,1)S(1)}, bf16[2,128,384]{1,2,0:T(8,128)(2,1)S(1)}, u32[]{:S(2)}, u32[]{:S(2)}) collective-permute-start(bf16[2,128,384]{1,2,0:T(8,128)(2,1)S(1)} %get-tuple-element.12), channel_id=1, source_target_pairs={{4,0},{8,4},{12,8},{5,1},{9,5},{13,9},{6,2},{10,6},{14,10},{7,3},{... | collective-permute-start | bytes 589832 | tf_op jit(solution)/shard_map/ppermute | solution.py:20
  48.3 4.4 copy-start.3
  48.3 4.4 copy-start.6
  150.4 187.9 %all-to-all-start = ((f32[4,1,524288]{2,1,0:T(1,128)}), f32[4,1,524288]{2,1,0:T(1,128)}, u32[]{:S(2)}, u32[]{:S(2)}) async-start(f32[4,1,524288]{2,1,0:T(1,128)} %reshape.77), calls=%async_computation | async-start | bytes 16777216 | tf_op jit(solution)/shard_map/all_to_all | solution.py:132
  715.1 10.4 %copy-start = (f32[2,32,128,128]{3,2,1,0:T(8,128)S(1)}, f32[2,32,128,128]{3,2,1,0:T(8,128)}, u32[]{:S(2)}) copy-start(f32[2,32,128,128]{3,2,1,0:T(8,128)} %slice.107) | copy-start | bytes 12582916
  725.5 8.7 %copy-start.8 = (f32[2,32,4,4096]{3,1,2,0:T(8,128)S(1)}, f32[2,32,4,4096]{3,1,2,0:T(8,128)}, u32[]{:S(2)}) copy-start(f32[2,32,4,4096]{3,1,2,0:T(8,128)} %get-tuple-element.7) | copy-start | bytes 12582916
  744.9 9.3 %copy-start.1 = (f32[2,32,128,128]{3,2,1,0:T(8,128)S(1)}, f32[2,32,128,128]{3,2,1,0:T(8,128)}, u32[]{:S(2)}) copy-start(f32[2,32,128,128]{3,2,1,0:T(8,128)} %slice.105) | copy-start | bytes 12582916
  754.2 7.1 copy-start.4
  761.2 4.3 copy-start.7
where the time goes:
time: 790 us; the launch traced here: 779 us
  local copies, waits for them, and re-layouts  211 us (27%)
  waiting for transfers between devices  187 us (24%)
  blocking collectives  187 us (24%)
  matrix products  117 us (15%)
  other arithmetic  64.9 us (8%)
  starting transfers between devices  11.9 us (2%)
    all_to_all x1, blocking collectives, on_device(): lax.all_to_all(filtered, 'tm', split_axis=1, concat_axis=2, tiled=True)  187 us
    all_to_all x1, waiting for transfers between devices, on_device(): lax.all_to_all(payload, 'tm', split_axis=2, concat_axis=1, tiled=True)  180 us
    unnamed x22, local copies, waits for them, and re-layouts  94.9 us
    all_to_all x2, local copies, waits for them, and re-layouts, on_device(): lax.all_to_all(payload, 'tm', split_axis=2, concat_axis=1, tiled=True)  29.4 us
    all_to_all x1, other arithmetic, on_device(): lax.all_to_all(payload, 'tm', split_axis=2, concat_axis=1, tiled=True)  28.4 us
    reshape x1, local copies, waits for them, and re-layouts, on_device(): jnp.concatenate([joined_real, joined_imag], axis=0)  26.7 us
  transfers between devices with their start and end apart: 3, of which 3 were waited for; matrix products, arithmetic and copies ran while one was open for 0% of the time, Pallas kernels for 0%

commit v1 on v0

--- a/solution.py
+++ b/solution.py
@@ -5,6 +5,13 @@
 from jax.sharding import PartitionSpec as P
 
 noise_level = 0.05
+
+
+def exchange_blocks(value, axis, split, join):
+    peers = lax.axis_size(axis)
+    blocks = jnp.stack(jnp.split(value, peers, axis=split), axis=0)
+    blocks = lax.all_to_all(blocks, axis, split_axis=0, concat_axis=0)
+    return jnp.concatenate(blocks, axis=join)
 
 
 def with_halo(cells, sides, width):
@@ -129,7 +136,7 @@
     payload = jnp.concatenate([joined_real, joined_imag], axis=0).reshape(
         2 * across, count, side * side
     )
-    gathered = lax.all_to_all(payload, "tm", split_axis=2, concat_axis=1, tiled=True)
+    gathered = exchange_blocks(payload, "tm", 2, 1)
     width = gathered.shape[2]
     start = lax.axis_index("tm") * width
     cutoff_local = lax.dynamic_slice_in_dim(cutoff.reshape(-1), start, width)

time: 790 us -> 637 us (0.81)
  local copies, waits for them, and re-layouts: 211 us -> 83.8 us
  other arithmetic: 64.9 us -> 40.4 us
    unnamed x22 -> x20, local copies, waits for them, and re-layouts: 94.9 us -> 5.5 us
    all_to_all x2 -> x0, local copies, waits for them, and re-layouts: 29.4 us -> none  [on_device(): lax.all_to_all(payload, 'tm', split_axis=2, concat_axis=1, tiled=True)]
    all_to_all x1 -> x0, other arithmetic: 28.4 us -> none  [on_device(): lax.all_to_all(payload, 'tm', split_axis=2, concat_axis=1, tiled=True)]
    reshape x1, local copies, waits for them, and re-layouts: 26.7 us -> 9.37 us  [on_device(): jnp.concatenate([joined_real, joined_imag], axis=0)]
    concatenate x0 -> x1, local copies, waits for them, and re-layouts: none -> 8.99 us  [on_device(): jnp.concatenate([joined_real, joined_imag], axis=0)]
where the time goes in v1:
time: 637 us; the launch traced here: 627 us
  blocking collectives  187 us (29%)
  waiting for transfers between devices  186 us (29%)
  matrix products  117 us (18%)
  local copies, waits for them, and re-layouts  83.8 us (13%)
  other arithmetic  40.4 us (6%)
  starting transfers between devices  11.9 us (2%)
    all_to_all x1, blocking collectives, on_device(): lax.all_to_all(filtered, 'tm', split_axis=1, concat_axis=2, tiled=True)  187 us
    all_to_all x1, waiting for transfers between devices, exchange_blocks(): blocks = lax.all_to_all(blocks, axis, split_axis=0, concat_axis=0)  179 us
    slice x3, local copies, waits for them, and re-layouts, on_device(): spectra_back[:across]  13.5 us
  transfers between devices with their start and end apart: 3, of which 3 were waited for; matrix products, arithmetic and copies ran while one was open for 0% of the time, Pallas kernels for 0%

profile of v1, /device:TPU:0, one launch (start us, length us, event | category | flops | bytes accessed | tf_op | source)
XLA Modules:
  0.0 626.9 jit_solution(2504989434783784409)
XLA Ops:
  0.0 3.2 copy.64
  3.2 2.2 copy.65
  5.5 5.0 collective-permute-start
  11.8 2.8 collective-permute-done
  14.6 4.1 collective-permute-done.1
  20.3 3.0 copy.66
  23.4 2.3 fusion.30
  25.7 2.2 fusion.32
  27.9 8.0 %fusion.10 = f32[2,36,128,128]{3,2,1,0:T(8,128)S(1)} fusion(f32[2,36,128,128]{3,2,1,0:T(8,128)S(1)} %fusion.30), kind=kOutput, calls=%fused_computation.19 | convolution fusion | flops 1813348352 | bytes 9437184 | tf_op jit(solution)/shard_map/ua,cnav->cnuv/dot_general | solution.py:51
  36.0 7.7 %fusion.12 = f32[2,36,128,128]{3,2,1,0:T(8,128)S(1)} fusion(f32[2,36,128,128]{3,2,1,0:T(8,128)S(1)} %fusion.30), kind=kOutput, calls=%fused_computation.21 | convolution fusion | flops 1813348352 | bytes 9437184 | tf_op jit(solution)/shard_map/ua,cnav->cnuv/dot_general | solution.py:48
  43.6 4.5 multiply_bitcast_fusion
  48.2 4.4 multiply_bitcast_fusion.1
  54.3 11.7 %slice_bitcast_fusion.8 = (f32[32,128,128]{1,2,0:T(8,128)}, f32[32,128,128]{1,2,0:T(8,128)}, f32[32,128,128]{1,2,0:T(8,128)}, f32[32,128,128]{1,2,0:T(8,128)}, f...) fusion(f32[1,36,128,128]{2,3,1,0:T(8,128)} %fusion.36), kind=kLoop, calls=%fused_computation.66 | loop fusion | flops 5242880 | bytes 23068672 | tf_op jit(solution)/shard_map/mul | solution.py:78
  65.9 9.8 %fusion.20 = (f32[2,32,128,128]{2,3,1,0:T(8,128)S(1)}, f32[2,32,128,128]{2,3,1,0:T(8,128)}) fusion(f32[2,36,128,128]{2,3,1,0:T(8,128)S(1)} %multiply_bitcast_fusion.1, f32[32,128,128]{1,2,0:T(8,128)} %get-tuple-element.18, f32[32,128,128]{1,2,0:T(8,128)} %get-tuple-element.19, f32[32,128,128]{1,2,0:T(8,128)} %get-tuple-element.20, ...), kind=kLoop, calls=%fused_computation.35 | loop fusion | flops 20971520 | bytes 62914560 | tf_op jit(solution)/shard_map/div | solution.py:86
  75.8 6.3 pad_maximum_fusion
  82.0 9.0 %copy.77 = f32[4,32,128,128]{3,2,1,0:T(8,128)} copy(f32[4,32,128,128]{2,3,1,0:T(8,128)} %pad_maximum_fusion) | data formatting | bytes 16777216 | tf_op jit(solution)/shard_map/concatenate | solution.py:136
  91.0 9.4 %reshape.58 = f32[4,32,16384]{2,1,0:T(8,128)} reshape(f32[4,32,128,128]{3,2,1,0:T(8,128)} %copy.77) | data formatting | bytes 16777216 | tf_op jit(solution)/shard_map/reshape | solution.py:136
  100.4 4.0 slice_bitcast_fusion.3
  104.4 3.6 pad_maximum_fusion.1
  108.0 5.6 all-to-all-start
  114.4 2.1 broadcast_compare_fusion
  116.4 179.4 %all-to-all-done = f32[4,4,32,4096]{3,2,1,0:T(8,128)} async-done(((f32[4,4,32,4096]{3,2,1,0:T(8,128)}), f32[4,4,32,4096]{3,2,1,0:T(8,128)}, u32[]{:S(2)}, u32[]{:S(2)}) %all-to-all-start) | async-done | bytes 8388640 | tf_op jit(solution)/shard_map/all_to_all | solution.py:13
  295.9 4.0 fusion.174
  300.3 6.8 %fusion.50 = f32[2,4096,128]{2,1,0:T(8,128)S(1)} fusion(f32[2,128,4096]{2,1,0:T(8,128)S(1)} %bitcast.145), kind=kOutput, calls=%fused_computation.88 | convolution fusion | flops 1610842112 | bytes 8388608 | tf_op jit(solution)/shard_map/wt,stk->swk/dot_general | solution.py:97
  307.6 7.2 %fusion.46 = f32[2,4096,128]{2,1,0:T(8,128)S(1)} fusion(f32[2,128,4096]{2,1,0:T(8,128)S(1)} %bitcast.147), kind=kOutput, calls=%fused_computation.84 | convolution fusion | flops 1610842112 | bytes 8388608 | tf_op jit(solution)/shard_map/wt,stk->swk/dot_general | solution.py:101
  314.8 6.9 %fusion.9 = f32[2,128,4096]{1,2,0:T(8,128)S(1)} fusion(f32[2,4096,128]{2,1,0:T(8,128)S(1)} %fusion.50, f32[2,128,4096]{2,1,0:T(8,128)S(1)} %bitcast.148, pred[128,4096]{0,1:T(8,128)(4,1)S(1)} %broadcast_compare_fusion), kind=kOutput, calls=%fused_computation.16 | convolution fusion | flops 1613987840 | bytes 13107200 | tf_op jit(solution)/shard_map/wt,stk->swk/dot_general | solution.py:98
  321.7 3.8 fusion.48
  325.5 6.9 %fusion.6 = f32[2,128,4096]{1,2,0:T(8,128)S(1)} fusion(f32[2,4096,128]{2,1,0:T(8,128)S(1)} %fusion.46, f32[2,128,4096]{2,1,0:T(8,128)S(1)} %bitcast.146, pred[128,4096]{0,1:T(8,128)(4,1)S(1)} %broadcast_compare_fusion), kind=kOutput, calls=%fused_computation.12 | convolution fusion | flops 1613987840 | bytes 13107200 | tf_op jit(solution)/shard_map/wt,stk->swk/dot_general | solution.py:102
  332.4 3.9 fusion.44
  336.3 3.7 fusion.3
  340.0 3.7 fusion.1
  343.6 3.8 pad_maximum_fusion.2
  347.4 10.3 %copy.92 = f32[4,128,4096]{2,0,1:T(4,128)} copy(f32[4,128,4096]{1,2,0:T(8,128)} %pad_maximum_fusion.2) | data formatting | bytes 16777216 | tf_op jit(solution)/shard_map/concatenate | solution.py:117
  357.7 187.1 %all_to_all.20 = f32[4,128,4096]{2,0,1:T(4,128)S(1)} all-to-all(f32[4,128,4096]{2,0,1:T(4,128)} %copy.92), channel_id=1, replica_groups=mesh['parts'=2,'tm'=4,'rows'=2,'cols'=2] {'tm'}, dimensions={1} | all-to-all | bytes 16777216 | tf_op jit(solution)/shard_map/all_to_all | solution.py:144
  544.8 4.9 copy.93
  549.6 2.8 fusion.173
  552.4 4.7 copy.97
  557.1 6.1 slice.107
  563.2 10.4 %fusion.61 = f32[2,32,128,128]{3,2,1,0:T(8,128)} fusion(f32[2,32,128,128]{3,2,1,0:T(8,128)} %slice.107), kind=kOutput, calls=%fused_computation.99 | convolution fusion | flops 1610842112 | bytes 8388608 | tf_op jit(solution)/shard_map/au,cnuv->cnav/dot_general | solution.py:63
  573.5 8.7 %fusion.55 = f32[2,32,128,128]{3,2,1,0:T(8,128)} fusion(f32[2,32,128,128]{3,2,1,0:T(8,128)S(1)} %copy-done), kind=kOutput, calls=%fused_computation.93 | convolution fusion | flops 1610842112 | bytes 8388608 | tf_op jit(solution)/shard_map/au,cnuv->cnav/dot_general | solution.py:60
  582.2 4.7 copy.94
  586.9 6.1 slice.105
  593.0 9.3 %fusion.53 = f32[2,32,128,128]{3,2,1,0:T(8,128)S(1)} fusion(f32[2,32,128,128]{3,2,1,0:T(8,128)} %slice.105), kind=kOutput, calls=%fused_computation.91 | convolution fusion | flops 1610842112 | bytes 8388608 | tf_op jit(solution)/shard_map/au,cnuv->cnav/dot_general | solution.py:63
  602.3 7.0 %fusion.63 = f32[2,32,128,128]{3,2,1,0:T(8,128)S(1)} fusion(f32[2,32,128,128]{3,2,1,0:T(8,128)S(1)} %copy-done.1), kind=kOutput, calls=%fused_computation.101 | convolution fusion | flops 1610842112 | bytes 8388608 | tf_op jit(solution)/shard_map/au,cnuv->cnav/dot_general | solution.py:60
  609.4 4.3 fusion.24
  613.7 4.9 multiply_bitcast_fusion.2
  618.6 2.2 copy.106
  620.8 5.6 copy.107
  (26 shorter events, 6.2 us)
Async XLA Ops:
  3.2 17.1 %copy-start.2 = (bf16[32,128,256]{1,2,0:T(8,128)(2,1)}, bf16[32,128,256]{1,2,0:T(8,128)(2,1)S(1)}, u32[]{:S(2)}) copy-start(bf16[32,128,256]{1,2,0:T(8,128)(2,1)S(1)} %copy.64) | copy-start | bytes 6291460
  5.5 14.8 %copy-start.5 = (bf16[32,128,128]{1,2,0:T(8,128)(2,1)}, bf16[32,128,128]{1,2,0:T(8,128)(2,1)S(1)}, u32[]{:S(2)}) copy-start(bf16[32,128,128]{1,2,0:T(8,128)(2,1)S(1)} %copy.65) | copy-start | bytes 3145732
  5.5 9.1 %collective-permute-start = (bf16[2,128,384]{1,2,0:T(8,128)(2,1)S(1)}, bf16[2,128,384]{1,2,0:T(8,128)(2,1)S(1)}, u32[]{:S(2)}, u32[]{:S(2)}) collective-permute-start(bf16[2,128,384]{1,2,0:T(8,128)(2,1)S(1)} %get-tuple-element.15), channel_id=1, source_target_pairs={{0,4},{4,8},{8,12},{1,5},{5,9},{9,13},{2,6},{6,10},{10,14},{3,7},{... | collective-permute-start | bytes 589832 | tf_op jit(solution)/shard_map/ppermute | solution.py:25
  10.5 8.3 %collective-permute-start.1 = (bf16[2,128,384]{1,2,0:T(8,128)(2,1)S(1)}, bf16[2,128,384]{1,2,0:T(8,128)(2,1)S(1)}, u32[]{:S(2)}, u32[]{:S(2)}) collective-permute-start(bf16[2,128,384]{1,2,0:T(8,128)(2,1)S(1)} %get-tuple-element.16), channel_id=1, source_target_pairs={{4,0},{8,4},{12,8},{5,1},{9,5},{13,9},{6,2},{10,6},{14,10},{7,3},{... | collective-permute-start | bytes 589832 | tf_op jit(solution)/shard_map/ppermute | solution.py:27
  48.2 4.4 copy-start.3
  48.2 4.4 copy-start.6
  108.0 187.9 %all-to-all-start = ((f32[4,4,32,4096]{3,2,1,0:T(8,128)}), f32[4,4,32,4096]{3,2,1,0:T(8,128)}, u32[]{:S(2)}, u32[]{:S(2)}) async-start(f32[4,4,32,4096]{3,2,1,0:T(8,128)} %pad_maximum_fusion.1), calls=%async_computation | async-start | bytes 16777216 | tf_op jit(solution)/shard_map/all_to_all | solution.py:13
  563.2 10.4 %copy-start = (f32[2,32,128,128]{3,2,1,0:T(8,128)S(1)}, f32[2,32,128,128]{3,2,1,0:T(8,128)}, u32[]{:S(2)}) copy-start(f32[2,32,128,128]{3,2,1,0:T(8,128)} %slice.107) | copy-start | bytes 12582916
  573.5 8.7 %copy-start.8 = (f32[2,32,4,4096]{3,1,2,0:T(8,128)S(1)}, f32[2,32,4,4096]{3,1,2,0:T(8,128)}, u32[]{:S(2)}) copy-start(f32[2,32,4,4096]{3,1,2,0:T(8,128)} %get-tuple-element.7) | copy-start | bytes 12582916
  593.0 9.3 %copy-start.1 = (f32[2,32,128,128]{3,2,1,0:T(8,128)S(1)}, f32[2,32,128,128]{3,2,1,0:T(8,128)}, u32[]{:S(2)}) copy-start(f32[2,32,128,128]{3,2,1,0:T(8,128)} %slice.105) | copy-start | bytes 12582916
  602.3 7.1 %copy-start.4 = (f32[2,32,128,128]{3,2,1,0:T(8,128)S(1)}, f32[2,32,128,128]{3,2,1,0:T(8,128)}, u32[]{:S(2)}) copy-start(f32[2,32,128,128]{3,2,1,0:T(8,128)} %fusion.61) | copy-start | bytes 12582916
  609.3 4.4 copy-start.7
